TPU v7x, 32 devices: a whole 2x2x4 slice. The times are simulated.
32 devices in a mesh: gx: 2 (over x), gy: 4 (over z), gz: 4 (over y, core).
Axes of the slice: x: 2, y: 2, z: 4, core: 2. Of those that a mesh axis runs over, the one named last changes fastest.
Arguments:
- volume: float32 [16, 8, 64, 512], P(None, 'gx', 'gy', 'gz'), may hold values from -26 to 26
- weight: float32 [16, 16, 3, 3, 3], replicated, may hold values from -0.3125 to 0.3125
- gamma: float32 [16], replicated, may hold values from 0.5 to 1.5
- beta: float32 [16], replicated, may hold values from -0.5 to 0.5
- cotangent: float32 [16, 8, 64, 512], P(None, 'gx', 'gy', 'gz'), may hold values from -6 to 6
Outputs:
- input_grad: float32 [16, 8, 64, 512], P(None, 'gx', 'gy', 'gz')
- weight_grad: float32 [16, 16, 3, 3, 3], replicated
- gamma_grad: float32 [16], replicated
- beta_grad: float32 [16], replicated
All inputs are finite; a program needn't handle non-finite values.
Results may differ from a plain program's by a relative error of at most 0.0003.
Values sent between devices are 32-bit elements; how exact they have to be, the bound alone decides.
No kernel may reach another device: no remote copies, remote signals or barrier semaphores. Data moves between devices by JAX's collectives and lax.ppermute only.
A program may use at most 64 MiB of HBM per device.

v0:
```python
import jax
import jax.numpy as jnp
from jax import lax
from jax.sharding import PartitionSpec as P


def with_halo(block, sides, width):
    for axis, dim in sides:
        count = lax.axis_size(axis)
        forward = [(i, i + 1) for i in range(count - 1)]
        forward.append((count - 1, 0))
        backward = [(target, source) for source, target in forward]
        low = lax.ppermute(
            lax.slice_in_dim(block, block.shape[dim] - width, None, axis=dim), axis, forward
        )
        high = lax.ppermute(lax.slice_in_dim(block, 0, width, axis=dim), axis, backward)
        block = jnp.concatenate([low, block, high], axis=dim)
    return block


def mix(kernel, slab):
    return jnp.einsum("oi,ixyz->oxyz", kernel, slab, precision=lax.Precision.HIGHEST)


def contract(left, slab):
    return jnp.einsum("oxyz,ixyz->oi", left, slab, precision=lax.Precision.HIGHEST)


def shards(volume, weight, gamma, beta, cotangent):
    chans, cells_x, cells_y, cells_z = volume.shape
    count = float(
        cells_x
        * cells_y
        * cells_z
        * lax.axis_size("gx")
        * lax.axis_size("gy")
        * lax.axis_size("gz")
    )
    padded = with_halo(volume, (("gx", 1), ("gy", 2), ("gz", 3)), 1)

    def window(source, first, second, third):
        return source[
            :, first : first + cells_x, second : second + cells_y, third : third + cells_z
        ]

    conv = jnp.zeros(volume.shape, jnp.float32)
    for first in range(3):
        for second in range(3):
            for third in range(3):
                conv = conv + mix(
                    weight[:, :, first, second, third], window(padded, first, second, third)
                )
    first_sum, square_sum = lax.psum(
        (jnp.sum(conv, axis=(1, 2, 3)), jnp.sum(conv * conv, axis=(1, 2, 3))), ("gx", "gy", "gz")
    )
    mean = first_sum / count
    var = square_sum / count - mean * mean
    centred = conv - mean[:, None, None, None]
    rstd = lax.rsqrt(var + 1e-05)
    normed = centred * rstd[:, None, None, None]
    act = gamma[:, None, None, None] * normed + beta[:, None, None, None]
    sig = jax.nn.sigmoid(act)
    act_grad = cotangent * sig * (1.0 + act * (1.0 - sig))
    scale = gamma * rstd
    gamma_grad, beta_grad = lax.psum(
        (jnp.sum(act_grad * normed, axis=(1, 2, 3)), jnp.sum(act_grad, axis=(1, 2, 3))),
        ("gx", "gy", "gz"),
    )
    conv_grad = scale[:, None, None, None] * (
        act_grad
        - (beta_grad / count)[:, None, None, None]
        - normed * (gamma_grad / count)[:, None, None, None]
    )
    pieces = []
    for first in range(3):
        for second in range(3):
            for third in range(3):
                pieces.append(contract(conv_grad, window(padded, first, second, third)))
    weight_grad = lax.psum(
        jnp.stack(pieces, axis=2).reshape(chans, chans, 3, 3, 3), ("gx", "gy", "gz")
    )
    grad_padded = with_halo(conv_grad, (("gx", 1), ("gy", 2), ("gz", 3)), 1)
    input_grad = jnp.zeros(volume.shape, jnp.float32)
    for first in range(3):
        for second in range(3):
            for third in range(3):
                input_grad = input_grad + mix(
                    weight[:, :, first, second, third].T,
                    window(grad_padded, 2 - first, 2 - second, 2 - third),
                )
    return (input_grad, weight_grad, gamma_grad, beta_grad)


def solution(mesh):
    return jax.shard_map(
        shards,
        mesh=mesh,
        in_specs=(P(None, "gx", "gy", "gz"), P(), P(), P(), P(None, "gx", "gy", "gz")),
        out_specs=(P(None, "gx", "gy", "gz"), P(), P(), P()),
        check_vma=False,
    )
```

profile of v0, /device:TPU:0, one launch (start us, length us, event | category | flops | bytes accessed | tf_op | source)
XLA Modules:
  0.0 250.0 jit_solution(15097560473422288166)
XLA Ops:
  0.6 1.1 fusion.319
  1.7 3.0 %collective-permute-start = (f32[16,1,16,128]{3,0,2,1:T(8,128)S(1)}, f32[16,1,16,128]{3,0,2,1:T(8,128)S(1)}, u32[]{:S(2)}, u32[]{:S(2)}) collective-permute-start(f32[16,1,16,128]{3,0,2,1:T(8,128)S(1)} %copy.207), channel_id=1, source_target_pairs={{0,16},{16,0},{1,17},{17,1},{2,18},{18,2},{3,19},{19,3},{4,20},{20... | collective-permute-start | bytes 393224 | tf_op jit(solution)/shard_map/ppermute | solution.py:13
  4.9 2.7 %fusion.206 = f32[16,4,16,128]{3,0,2,1:T(8,128)} fusion(f32[16,16,3,3,3]{1,0,4,3,2:T(8,128)} %param.6, f32[16,4,16,128]{3,2,1,0:T(8,128)} %param.5), kind=kOutput, calls=%fused_computation.290 | convolution fusion | flops 25165824 | bytes 1056768 | tf_op jit(solution)/shard_map/oi,ixyz->oxyz/dot_general | solution.py:22
  7.6 1.5 collective-permute-done
  9.5 1.6 collective-permute-done.1
  11.1 1.9 collective-permute-start.2
  13.0 2.1 collective-permute-start.3
  15.1 2.1 fusion.225
  17.2 2.1 convolution_bitcast_fusion.4
  21.0 1.9 collective-permute-start.5
  22.9 2.1 fusion.85
  25.0 2.1 fusion.86
  27.1 2.1 fusion.87
  29.1 2.1 convolution_bitcast_fusion.3
  31.2 2.1 convolution_bitcast_fusion.5
  33.3 2.1 convolution_bitcast_fusion.6
  36.1 1.6 copy.51
  37.7 1.8 maximum_maximum_fusion
  47.1 1.1 convolution_bitcast_fusion.18
  50.1 1.0 fusion.44
  51.6 1.2 fusion.312
  52.8 38.9 %all-reduce.1 = (f32[16]{0:T(128)S(1)}, f32[16]{0:T(128)S(1)}) all-reduce(f32[16]{0:T(128)S(1)} %get-tuple-element.15, f32[16]{0:T(128)S(1)} %get-tuple-element.14), channel_id=1, replica_groups=mesh['gx'=2,'gy'=4,'gz'=4] {'gx','gy','gz'}, use_global_device_ids=true, to_apply=%region_1.0 | all-reduce | flops 32 | bytes 256 | tf_op jit(solution)/shard_map/psum | solution.py:53
  91.7 2.4 fusion.311
  94.1 40.5 %all-reduce = (f32[16]{0:T(128)S(1)}, f32[16]{0:T(128)S(1)}) all-reduce(f32[16]{0:T(128)S(1)} %get-tuple-element.13, f32[16]{0:T(128)S(1)} %get-tuple-element.12), channel_id=1, replica_groups=mesh['gx'=2,'gy'=4,'gz'=4] {'gx','gy','gz'}, use_global_device_ids=true, to_apply=%region_7.0 | all-reduce | flops 32 | bytes 256 | tf_op jit(solution)/shard_map/psum | solution.py:65
  134.6 1.4 subtract_multiply_fusion
  138.3 0.9 fusion.75
  139.2 0.8 fusion.74
  140.8 0.9 fusion.72
  141.7 0.8 fusion.71
  143.3 0.9 fusion.69
  144.2 0.8 fusion.68
  145.8 0.9 fusion.66
  147.4 1.0 fusion.64
  148.4 0.9 fusion.63
  149.3 0.8 fusion.62
  150.9 0.9 fusion.60
  151.8 0.8 fusion.59
  153.4 0.9 fusion.57
  154.3 0.8 fusion.56
  155.1 0.9 fusion.55
  156.1 0.9 fusion.54
  158.6 0.9 fusion.51
  160.2 41.9 %psum.39 = f32[16,16,3,3,3]{1,0,4,3,2:T(8,128)} all-reduce(f32[16,16,3,3,3]{1,0,4,3,2:T(8,128)} %bitcast.644), channel_id=1, replica_groups=mesh['gx'=2,'gy'=4,'gz'=4] {'gx','gy','gz'}, use_global_device_ids=true, to_apply=%region_8.0 | all-reduce | flops 6912 | bytes 55296 | tf_op jit(solution)/shard_map/psum | solution.py:79
  202.1 1.6 collective-permute-start.6
  204.2 1.4 fusion.204
  205.6 2.5 collective-permute-done.6
  208.0 1.4 collective-permute-done.7
  209.4 2.2 collective-permute-start.9
  211.7 1.4 fusion.78
  213.7 3.9 %collective-permute-done.8 = f32[16,6,1,128]{3,0,2,1:T(8,128)S(1)} collective-permute-done((f32[16,6,1,128]{3,0,2,1:T(8,128)S(1)}, f32[16,6,1,128]{3,0,2,1:T(8,128)S(1)}, u32[]{:S(2)}, u32[]{:S(2)}) %collective-permute-start.8) | collective-permute-done | bytes 49184 | tf_op jit(solution)/shard_map/ppermute | solution.py:13
  217.6 1.2 fusion.315
  218.8 1.8 copy.56
  221.9 1.4 fusion.177
  223.3 1.4 fusion.175
  224.7 1.4 fusion.176
  226.1 1.4 fusion.174
  227.5 1.4 convolution_bitcast_fusion.2
  228.9 1.4 convolution_bitcast_fusion
  230.3 1.6 copy.57
  231.9 1.6 copy.61
  233.5 2.0 pad_maximum_fusion.3
  246.5 1.1 fusion.46
  247.8 1.0 fusion.48
  248.8 1.0 copy.88
  (142 shorter events, 35.3 us)
Async XLA Ops:
  0.6 8.5 %copy-start.2 = (f32[16,4,16,128]{3,2,1,0:T(8,128)S(1)}, f32[16,4,16,128]{3,2,1,0:T(8,128)}, u32[]{:S(2)}) copy-start(f32[16,4,16,128]{3,2,1,0:T(8,128)} %param.5) | copy-start | bytes 1572868
  1.7 7.4 %collective-permute-start = (f32[16,1,16,128]{3,0,2,1:T(8,128)S(1)}, f32[16,1,16,128]{3,0,2,1:T(8,128)S(1)}, u32[]{:S(2)}, u32[]{:S(2)}) collective-permute-start(f32[16,1,16,128]{3,0,2,1:T(8,128)S(1)} %copy.207), channel_id=1, source_target_pairs={{0,16},{16,0},{1,17},{17,1},{2,18},{18,2},{3,19},{19,3},{4,20},{20... | collective-permute-start | bytes 393224 | tf_op jit(solution)/shard_map/ppermute | solution.py:13
  4.8 6.3 %collective-permute-start.1 = (f32[16,1,16,128]{3,0,2,1:T(8,128)S(1)}, f32[16,1,16,128]{3,0,2,1:T(8,128)S(1)}, u32[]{:S(2)}, u32[]{:S(2)}) collective-permute-start(f32[16,1,16,128]{3,0,2,1:T(8,128)S(1)} %copy.208), channel_id=1, source_target_pairs={{16,0},{0,16},{17,1},{1,17},{18,2},{2,18},{19,3},{3,19},{20,4},{4,... | collective-permute-start | bytes 393224 | tf_op jit(solution)/shard_map/ppermute | solution.py:16
  9.5 9.7 %copy-start.7 = (f32[16,5,16,128]{3,0,2,1:T(8,128)}, f32[16,5,16,128]{3,0,2,1:T(8,128)S(1)}, u32[]{:S(2)}) copy-start(f32[16,5,16,128]{3,0,2,1:T(8,128)S(1)} %get-tuple-element.37) | copy-start | bytes 1966084
  11.1 8.1 %copy-start.5 = (f32[16,5,16,128]{3,0,2,1:T(8,128)}, f32[16,5,16,128]{3,0,2,1:T(8,128)S(1)}, u32[]{:S(2)}) copy-start(f32[16,5,16,128]{3,0,2,1:T(8,128)S(1)} %get-tuple-element.44) | copy-start | bytes 1966084
  11.1 8.1 %collective-permute-start.2 = (f32[16,6,1,128]{3,0,2,1:T(8,128)S(1)}, f32[16,6,1,128]{3,0,2,1:T(8,128)S(1)}, u32[]{:S(2)}, u32[]{:S(2)}) collective-permute-start(f32[16,6,1,128]{3,0,2,1:T(8,128)S(1)} %get-tuple-element.33), channel_id=1, source_target_pairs={{0,4},{4,8},{8,12},{12,0},{1,5},{5,9},{9,13},{13,1},{2,6},{6,10},{... | collective-permute-start | bytes 147464 | tf_op jit(solution)/shard_map/ppermute | solution.py:13
  13.0 6.2 %collective-permute-start.3 = (f32[16,6,1,128]{3,0,2,1:T(8,128)S(1)}, f32[16,6,1,128]{3,0,2,1:T(8,128)S(1)}, u32[]{:S(2)}, u32[]{:S(2)}) collective-permute-start(f32[16,6,1,128]{3,0,2,1:T(8,128)S(1)} %get-tuple-element.34), channel_id=1, source_target_pairs={{4,0},{8,4},{12,8},{0,12},{5,1},{9,5},{13,9},{1,13},{6,2},{10,6},{... | collective-permute-start | bytes 147464 | tf_op jit(solution)/shard_map/ppermute | solution.py:16
  20.3 15.1 %collective-permute-start.4 = (f32[16,6,18,1]{2,0,3,1:T(8,128)S(1)}, f32[16,6,18,1]{2,0,3,1:T(8,128)S(1)}, u32[]{:S(2)}, u32[]{:S(2)}) collective-permute-start(f32[16,6,18,1]{2,0,3,1:T(8,128)S(1)} %copy.48), channel_id=1, source_target_pairs={{0,1},{1,2},{2,3},{3,0},{4,5},{5,6},{6,7},{7,4},{8,9},{9,10},{10,1... | collective-permute-start | bytes 20744 | tf_op jit(solution)/shard_map/ppermute | solution.py:13
  21.0 15.1 %collective-permute-start.5 = (f32[16,6,18,1]{2,0,3,1:T(8,128)S(1)}, f32[16,6,18,1]{2,0,3,1:T(8,128)S(1)}, u32[]{:S(2)}, u32[]{:S(2)}) collective-permute-start(f32[16,6,18,1]{2,0,3,1:T(8,128)S(1)} %copy.50), channel_id=1, source_target_pairs={{1,0},{2,1},{3,2},{0,3},{5,4},{6,5},{7,6},{4,7},{9,8},{10,9},{11,1... | collective-permute-start | bytes 20744 | tf_op jit(solution)/shard_map/ppermute | solution.py:16
  37.7 1.8 copy-start.26
  39.5 11.6 %copy-start = (f32[16,6,18,129]{3,0,2,1:T(8,128)}, f32[16,6,18,129]{3,0,2,1:T(8,128)S(1)}, u32[]{:S(2)}) copy-start(f32[16,6,18,129]{3,0,2,1:T(8,128)S(1)} %get-tuple-element.28) | copy-start | bytes 2674948
  48.2 1.9 copy-start.11
  48.2 1.9 copy-start.12
  48.2 1.9 copy-start.23
  48.2 1.9 copy-start.24
  48.2 1.9 copy-start.25
  50.1 1.0 copy-start.9
  50.1 1.2 copy-start.17
  50.1 1.3 copy-start.18
  50.1 1.5 copy-start.19
  51.6 40.1 %copy-start.31 = (f32[16]{0:T(128)S(1)}, f32[16]{0:T(128)}, u32[]{:S(2)}) copy-start(f32[16]{0:T(128)} %param.7) | copy-start | bytes 196
  51.6 40.1 %copy-start.32 = (f32[16]{0:T(128)S(1)}, f32[16]{0:T(128)}, u32[]{:S(2)}) copy-start(f32[16]{0:T(128)} %param.8) | copy-start | bytes 196
  52.8 81.8 %copy-start.4 = (f32[16,4,16,128]{3,0,2,1:T(8,128)}, f32[16,4,16,128]{3,0,2,1:T(8,128)S(1)}, u32[]{:S(2)}) copy-start(f32[16,4,16,128]{3,0,2,1:T(8,128)S(1)} %get-tuple-element.47) | copy-start | bytes 1572868
  134.6 3.7 %copy-start.33 = (f32[16]{0:T(128)}, f32[16]{0:T(128)S(1)}, u32[]{:S(2)}) copy-start(f32[16]{0:T(128)S(1)} %get-tuple-element.16) | copy-start | bytes 196
  134.6 3.7 %copy-start.34 = (f32[16]{0:T(128)}, f32[16]{0:T(128)S(1)}, u32[]{:S(2)}) copy-start(f32[16]{0:T(128)S(1)} %get-tuple-element.17) | copy-start | bytes 196
  136.0 2.3 copy-start.1
  137.5 2.5 %copy-start.8 = (f32[16,5,16,128]{3,0,2,1:T(8,128)S(1)}, f32[16,5,16,128]{3,0,2,1:T(8,128)}, u32[]{:S(2)}) copy-start(f32[16,5,16,128]{3,0,2,1:T(8,128)} %copy-done.7) | copy-start | bytes 1966084
  145.0 2.5 copy-start.3
  152.6 2.5 %copy-start.6 = (f32[16,5,16,128]{3,0,2,1:T(8,128)S(1)}, f32[16,5,16,128]{3,0,2,1:T(8,128)}, u32[]{:S(2)}) copy-start(f32[16,5,16,128]{3,0,2,1:T(8,128)} %copy-done.5) | copy-start | bytes 1966084
  157.0 47.2 %copy-start.27 = (f32[16,16,3,3,3]{1,0,4,3,2:T(8,128)S(1)}, f32[16,16,3,3,3]{1,0,4,3,2:T(8,128)}, u32[]{:S(2)}) copy-start(f32[16,16,3,3,3]{1,0,4,3,2:T(8,128)} %param.6) | copy-start | bytes 82948
  157.8 44.3 %copy-start.30 = (f32[16,1,16,128]{3,0,2,1:T(8,128)S(1)}, f32[16,1,16,128]{3,0,2,1:T(8,128)}, u32[]{:S(2)}) copy-start(f32[16,1,16,128]{3,0,2,1:T(8,128)} %get-tuple-element.35) | copy-start | bytes 393220
  157.8 45.9 %copy-start.29 = (f32[16,1,16,128]{3,0,2,1:T(8,128)S(1)}, f32[16,1,16,128]{3,0,2,1:T(8,128)}, u32[]{:S(2)}) copy-start(f32[16,1,16,128]{3,0,2,1:T(8,128)} %get-tuple-element.36) | copy-start | bytes 393220
  159.5 0.7 copy-start.28
  202.1 5.9 %collective-permute-start.6 = (f32[16,1,16,128]{3,0,2,1:T(8,128)S(1)}, f32[16,1,16,128]{3,0,2,1:T(8,128)S(1)}, u32[]{:S(2)}, u32[]{:S(2)}) collective-permute-start(f32[16,1,16,128]{3,0,2,1:T(8,128)S(1)} %copy-done.30), channel_id=1, source_target_pairs={{0,16},{16,0},{1,17},{17,1},{2,18},{18,2},{3,19},{19,3},{4,20},{20... | collective-permute-start | bytes 393224 | tf_op jit(solution)/shard_map/ppermute | solution.py:13
  203.7 5.7 %collective-permute-start.7 = (f32[16,1,16,128]{3,0,2,1:T(8,128)S(1)}, f32[16,1,16,128]{3,0,2,1:T(8,128)S(1)}, u32[]{:S(2)}, u32[]{:S(2)}) collective-permute-start(f32[16,1,16,128]{3,0,2,1:T(8,128)S(1)} %copy-done.29), channel_id=1, source_target_pairs={{16,0},{0,16},{17,1},{1,17},{18,2},{2,18},{19,3},{3,19},{20,4},{4,... | collective-permute-start | bytes 393224 | tf_op jit(solution)/shard_map/ppermute | solution.py:16
  209.4 4.2 %collective-permute-start.9 = (f32[16,6,1,128]{3,0,2,1:T(8,128)S(1)}, f32[16,6,1,128]{3,0,2,1:T(8,128)S(1)}, u32[]{:S(2)}, u32[]{:S(2)}) collective-permute-start(f32[16,6,1,128]{3,0,2,1:T(8,128)S(1)} %get-tuple-element.32), channel_id=1, source_target_pairs={{4,0},{8,4},{12,8},{0,12},{5,1},{9,5},{13,9},{1,13},{6,2},{10,6},{... | collective-permute-start | bytes 147464 | tf_op jit(solution)/shard_map/ppermute | solution.py:16
  211.7 5.9 %collective-permute-start.8 = (f32[16,6,1,128]{3,0,2,1:T(8,128)S(1)}, f32[16,6,1,128]{3,0,2,1:T(8,128)S(1)}, u32[]{:S(2)}, u32[]{:S(2)}) collective-permute-start(f32[16,6,1,128]{3,0,2,1:T(8,128)S(1)} %get-tuple-element.31), channel_id=1, source_target_pairs={{0,4},{4,8},{8,12},{12,0},{1,5},{5,9},{9,13},{13,1},{2,6},{6,10},{... | collective-permute-start | bytes 147464 | tf_op jit(solution)/shard_map/ppermute | solution.py:13
  220.7 9.7 %collective-permute-start.10 = (f32[16,6,18,1]{2,0,3,1:T(8,128)S(1)}, f32[16,6,18,1]{2,0,3,1:T(8,128)S(1)}, u32[]{:S(2)}, u32[]{:S(2)}) collective-permute-start(f32[16,6,18,1]{2,0,3,1:T(8,128)S(1)} %copy.56), channel_id=1, source_target_pairs={{1,0},{2,1},{3,2},{0,3},{5,4},{6,5},{7,6},{4,7},{9,8},{10,9},{11,1... | collective-permute-start | bytes 20744 | tf_op jit(solution)/shard_map/ppermute | solution.py:16
  221.4 10.6 %collective-permute-start.11 = (f32[16,6,18,1]{2,0,3,1:T(8,128)S(1)}, f32[16,6,18,1]{2,0,3,1:T(8,128)S(1)}, u32[]{:S(2)}, u32[]{:S(2)}) collective-permute-start(f32[16,6,18,1]{2,0,3,1:T(8,128)S(1)} %copy.60), channel_id=1, source_target_pairs={{0,1},{1,2},{2,3},{3,0},{4,5},{5,6},{6,7},{7,4},{8,9},{9,10},{10,1... | collective-permute-start | bytes 20744 | tf_op jit(solution)/shard_map/ppermute | solution.py:13
  244.1 2.3 copy-start.10
  244.1 2.3 copy-start.13
  244.1 2.3 copy-start.20
  244.3 2.1 copy-start.21
  244.3 2.1 copy-start.22
  246.4 1.1 copy-start.14
  246.4 1.2 copy-start.15
  246.4 1.3 copy-start.16
where the time goes:
time: 255 us; the launch traced here: 250 us
  blocking collectives  121 us (47%)
  matrix products  78.7 us (31%)
  local copies, waits for them, and re-layouts  15.7 us (6%)
  starting transfers between devices  13.8 us (5%)
  waiting for transfers between devices  10.9 us (4%)
  other arithmetic  7.77 us (3%)
    dot_general x54, matrix products, mix(): jnp.einsum('oi,ixyz->oxyz', kernel, slab, precision=lax.Precision.HIGHEST)  56 us
    psum x1, blocking collectives, shards(): lax.psum(jnp.stack(pieces, axis=2).reshape(chans, chans, 3, 3, 3), ('gx',...  41.9 us
    psum x1, blocking collectives, shards(): lax.psum((jnp.sum(act_grad * normed, axis=(1, 2, 3)), jnp.sum(act_grad, a...  40.5 us
    psum x1, blocking collectives, shards(): lax.psum((jnp.sum(conv, axis=(1, 2, 3)), jnp.sum(conv * conv, axis=(1, 2,...  38.9 us
    dot_general x27, matrix products, contract(): jnp.einsum('oxyz,ixyz->oi', left, slab, precision=lax.Precision.HIGHEST)  22.7 us
    ppermute x6, waiting for transfers between devices, with_halo(): lax.ppermute(lax.slice_in_dim(block, block.shape[dim] - width, None, axis...  7.88 us
    ppermute x6, starting transfers between devices, with_halo(): lax.ppermute(lax.slice_in_dim(block, block.shape[dim] - width, None, axis...  7.03 us
    ppermute x6, starting transfers between devices, with_halo(): lax.ppermute(lax.slice_in_dim(block, 0, width, axis=dim), axis, backward)  6.81 us
  transfers between devices with their start and end apart: 12, of which 5 were waited for; matrix products, arithmetic and copies ran while one was open for 14% of the time, Pallas kernels for 0%

commit v1 on v0

--- a/solution.py
+++ b/solution.py
@@ -76,9 +76,9 @@
         for second in range(3):
             for third in range(3):
                 pieces.append(contract(conv_grad, window(padded, first, second, third)))
-    weight_grad = lax.psum(
-        jnp.stack(pieces, axis=2).reshape(chans, chans, 3, 3, 3), ("gx", "gy", "gz")
-    )
+    part = jnp.stack(pieces, axis=2).reshape(chans, chans, 3, 3, 3)
+    terms = lax.all_gather(part, ("gx", "gy", "gz"), axis=0, tiled=False)
+    weight_grad = terms.sum(axis=0)
     grad_padded = with_halo(conv_grad, (("gx", 1), ("gy", 2), ("gz", 3)), 1)
     input_grad = jnp.zeros(volume.shape, jnp.float32)
     for first in range(3):

time: 255 us -> 307 us (1.20)
  blocking collectives: 121 us -> 175 us
  waiting for transfers between devices: 10.9 us -> 6.18 us
  other arithmetic: 7.77 us -> 12 us
    all_gather x0 -> x1, blocking collectives: none -> 96.1 us  [shards(): terms = lax.all_gather(part, ('gx', 'gy', 'gz'), axis=0, tiled=False)]
    psum x1 -> x0, blocking collectives: 41.9 us -> none  [shards(): lax.psum(jnp.stack(pieces, axis=2).reshape(chans, chans, 3, 3, 3), ('gx',...]
    ppermute x6, waiting for transfers between devices: 7.88 us -> 2.88 us  [with_halo(): lax.ppermute(lax.slice_in_dim(block, block.shape[dim] - width, None, axis...]
    reduce_sum x0 -> x1, other arithmetic: none -> 4.19 us  [shards(): weight_grad = terms.sum(axis=0)]
  transfers between devices with their start and end apart: 12 -> 12, of which waited for: 5 -> 5; matrix products, arithmetic and copies ran while one was open for 14% -> 13% of each run, Pallas kernels for 0% -> 0%
where the time goes in v1:
time: 307 us; the launch traced here: 303 us
  blocking collectives  175 us (57%)
  matrix products  78.8 us (26%)
  local copies, waits for them, and re-layouts  15 us (5%)
  starting transfers between devices  13.7 us (4%)
  other arithmetic  12 us (4%)
  waiting for transfers between devices  6.18 us (2%)
    all_gather x1, blocking collectives, shards(): terms = lax.all_gather(part, ('gx', 'gy', 'gz'), axis=0, tiled=False)  96.1 us
    dot_general x54, matrix products, mix(): jnp.einsum('oi,ixyz->oxyz', kernel, slab, precision=lax.Precision.HIGHEST)  56.1 us
    psum x1, blocking collectives, shards(): lax.psum((jnp.sum(act_grad * normed, axis=(1, 2, 3)), jnp.sum(act_grad, a...  40.5 us
    psum x1, blocking collectives, shards(): lax.psum((jnp.sum(conv, axis=(1, 2, 3)), jnp.sum(conv * conv, axis=(1, 2,...  38.9 us
    dot_general x27, matrix products, contract(): jnp.einsum('oxyz,ixyz->oi', left, slab, precision=lax.Precision.HIGHEST)  22.7 us
    ppermute x6, starting transfers between devices, with_halo(): lax.ppermute(lax.slice_in_dim(block, block.shape[dim] - width, None, axis...  7.47 us
    ppermute x6, starting transfers between devices, with_halo(): lax.ppermute(lax.slice_in_dim(block, 0, width, axis=dim), axis, backward)  6.21 us
  transfers between devices with their start and end apart: 12, of which 5 were waited for; matrix products, arithmetic and copies ran while one was open for 13% of the time, Pallas kernels for 0%

profile of v1, /device:TPU:0, one launch (start us, length us, event | category | flops | bytes accessed | tf_op | source)
XLA Modules:
  0.0 302.9 jit_solution(798166474594075779)
XLA Ops:
  0.6 1.1 fusion.319
  1.7 3.0 %collective-permute-start = (f32[16,1,16,128]{3,0,2,1:T(8,128)S(1)}, f32[16,1,16,128]{3,0,2,1:T(8,128)S(1)}, u32[]{:S(2)}, u32[]{:S(2)}) collective-permute-start(f32[16,1,16,128]{3,0,2,1:T(8,128)S(1)} %copy.207), channel_id=1, source_target_pairs={{0,16},{16,0},{1,17},{17,1},{2,18},{18,2},{3,19},{19,3},{4,20},{20... | collective-permute-start | bytes 393224 | tf_op jit(solution)/shard_map/ppermute | solution.py:13
  4.9 2.7 fusion.206
  7.6 1.5 collective-permute-done
  9.5 1.6 collective-permute-done.1
  11.1 1.9 collective-permute-start.2
  13.0 2.1 collective-permute-start.3
  15.1 2.1 fusion.225
  17.2 2.1 convolution_bitcast_fusion.4
  21.0 1.9 collective-permute-start.5
  23.0 2.1 fusion.85
  25.0 2.0 fusion.86
  27.1 2.1 fusion.87
  29.2 2.1 convolution_bitcast_fusion.3
  31.2 2.1 convolution_bitcast_fusion.5
  33.3 2.1 convolution_bitcast_fusion.6
  36.1 1.6 copy.51
  37.7 1.8 maximum_maximum_fusion
  47.1 1.1 convolution_bitcast_fusion.18
  50.2 1.0 fusion.44
  51.6 1.2 fusion.312
  52.8 38.9 %all-reduce.1 = (f32[16]{0:T(128)S(1)}, f32[16]{0:T(128)S(1)}) all-reduce(f32[16]{0:T(128)S(1)} %get-tuple-element.15, f32[16]{0:T(128)S(1)} %get-tuple-element.14), channel_id=1, replica_groups=mesh['gx'=2,'gy'=4,'gz'=4] {'gx','gy','gz'}, use_global_device_ids=true, to_apply=%region_1.0 | all-reduce | flops 32 | bytes 256 | tf_op jit(solution)/shard_map/psum | solution.py:53
  91.7 2.4 fusion.311
  94.1 40.5 %all-reduce = (f32[16]{0:T(128)S(1)}, f32[16]{0:T(128)S(1)}) all-reduce(f32[16]{0:T(128)S(1)} %get-tuple-element.13, f32[16]{0:T(128)S(1)} %get-tuple-element.12), channel_id=1, replica_groups=mesh['gx'=2,'gy'=4,'gz'=4] {'gx','gy','gz'}, use_global_device_ids=true, to_apply=%region_7.0 | all-reduce | flops 32 | bytes 256 | tf_op jit(solution)/shard_map/psum | solution.py:65
  134.6 1.4 subtract_multiply_fusion
  138.3 0.9 fusion.75
  139.2 0.8 fusion.74
  140.8 0.9 fusion.72
  141.7 0.8 fusion.71
  143.3 0.9 fusion.69
  144.2 0.8 fusion.68
  145.8 0.9 fusion.66
  146.7 0.8 fusion.65
  147.5 1.0 fusion.64
  148.5 0.9 fusion.63
  149.4 0.8 fusion.62
  151.0 0.9 fusion.60
  151.9 0.8 fusion.59
  153.5 0.9 fusion.57
  155.1 1.0 fusion.55
  156.1 0.9 fusion.54
  158.6 0.9 fusion.51
  159.5 96.1 %all_gather.3 = f32[32,16,16,3,3,3]{2,1,5,4,3,0:T(8,128)} all-gather(f32[1,16,16,3,3,3]{2,1,5,4,3,0:T(8,128)S(1)} %bitcast.644), channel_id=1, replica_groups=mesh['gx'=2,'gy'=4,'gz'=4] {'gx','gy','gz'}, dimensions={0}, use_global_device_ids=true | all-gather | bytes 912384 | tf_op jit(solution)/shard_map/all_gather | solution.py:80
  255.6 2.0 collective-permute-start.7
  257.6 4.2 %reduce_sum.49 = f32[16,16,3,3,3]{1,0,4,3,2:T(8,128)} reduce(f32[32,16,16,3,3,3]{2,1,5,4,3,0:T(8,128)} %all_gather.3, f32[]{:T(128)} %constant.8.clone.1), dimensions={0}, to_apply=%region_8.0 | reduce | flops 214272 | bytes 912388 | tf_op jit(solution)/shard_map/reduce_sum | solution.py:81
  261.8 1.4 fusion.204
  263.2 1.2 collective-permute-done.7
  264.5 2.0 collective-permute-start.8
  266.5 1.4 fusion.78
  269.1 1.3 collective-permute-done.8
  270.5 1.2 fusion.315
  271.7 1.8 copy.56
  274.8 1.4 fusion.177
  276.2 1.4 fusion.175
  277.6 1.4 fusion.176
  279.0 1.4 fusion.174
  280.4 1.4 convolution_bitcast_fusion.2
  281.8 1.4 convolution_bitcast_fusion
  283.2 1.6 copy.57
  284.8 1.6 copy.61
  286.4 2.0 pad_maximum_fusion.3
  299.4 1.1 fusion.46
  300.7 1.0 fusion.48
  301.7 1.0 copy.88
  (137 shorter events, 34.7 us)
Async XLA Ops:
  0.6 8.5 %copy-start.2 = (f32[16,4,16,128]{3,2,1,0:T(8,128)S(1)}, f32[16,4,16,128]{3,2,1,0:T(8,128)}, u32[]{:S(2)}) copy-start(f32[16,4,16,128]{3,2,1,0:T(8,128)} %param.5) | copy-start | bytes 1572868
  1.7 7.4 %collective-permute-start = (f32[16,1,16,128]{3,0,2,1:T(8,128)S(1)}, f32[16,1,16,128]{3,0,2,1:T(8,128)S(1)}, u32[]{:S(2)}, u32[]{:S(2)}) collective-permute-start(f32[16,1,16,128]{3,0,2,1:T(8,128)S(1)} %copy.207), channel_id=1, source_target_pairs={{0,16},{16,0},{1,17},{17,1},{2,18},{18,2},{3,19},{19,3},{4,20},{20... | collective-permute-start | bytes 393224 | tf_op jit(solution)/shard_map/ppermute | solution.py:13
  4.8 6.3 %collective-permute-start.1 = (f32[16,1,16,128]{3,0,2,1:T(8,128)S(1)}, f32[16,1,16,128]{3,0,2,1:T(8,128)S(1)}, u32[]{:S(2)}, u32[]{:S(2)}) collective-permute-start(f32[16,1,16,128]{3,0,2,1:T(8,128)S(1)} %copy.208), channel_id=1, source_target_pairs={{16,0},{0,16},{17,1},{1,17},{18,2},{2,18},{19,3},{3,19},{20,4},{4,... | collective-permute-start | bytes 393224 | tf_op jit(solution)/shard_map/ppermute | solution.py:16
  9.5 9.8 %copy-start.7 = (f32[16,5,16,128]{3,0,2,1:T(8,128)}, f32[16,5,16,128]{3,0,2,1:T(8,128)S(1)}, u32[]{:S(2)}) copy-start(f32[16,5,16,128]{3,0,2,1:T(8,128)S(1)} %get-tuple-element.37) | copy-start | bytes 1966084
  11.1 8.1 %copy-start.5 = (f32[16,5,16,128]{3,0,2,1:T(8,128)}, f32[16,5,16,128]{3,0,2,1:T(8,128)S(1)}, u32[]{:S(2)}) copy-start(f32[16,5,16,128]{3,0,2,1:T(8,128)S(1)} %get-tuple-element.44) | copy-start | bytes 1966084
  11.1 8.1 %collective-permute-start.2 = (f32[16,6,1,128]{3,0,2,1:T(8,128)S(1)}, f32[16,6,1,128]{3,0,2,1:T(8,128)S(1)}, u32[]{:S(2)}, u32[]{:S(2)}) collective-permute-start(f32[16,6,1,128]{3,0,2,1:T(8,128)S(1)} %get-tuple-element.33), channel_id=1, source_target_pairs={{0,4},{4,8},{8,12},{12,0},{1,5},{5,9},{9,13},{13,1},{2,6},{6,10},{... | collective-permute-start | bytes 147464 | tf_op jit(solution)/shard_map/ppermute | solution.py:13
  13.0 6.2 %collective-permute-start.3 = (f32[16,6,1,128]{3,0,2,1:T(8,128)S(1)}, f32[16,6,1,128]{3,0,2,1:T(8,128)S(1)}, u32[]{:S(2)}, u32[]{:S(2)}) collective-permute-start(f32[16,6,1,128]{3,0,2,1:T(8,128)S(1)} %get-tuple-element.34), channel_id=1, source_target_pairs={{4,0},{8,4},{12,8},{0,12},{5,1},{9,5},{13,9},{1,13},{6,2},{10,6},{... | collective-permute-start | bytes 147464 | tf_op jit(solution)/shard_map/ppermute | solution.py:16
  20.3 15.1 %collective-permute-start.4 = (f32[16,6,18,1]{2,0,3,1:T(8,128)S(1)}, f32[16,6,18,1]{2,0,3,1:T(8,128)S(1)}, u32[]{:S(2)}, u32[]{:S(2)}) collective-permute-start(f32[16,6,18,1]{2,0,3,1:T(8,128)S(1)} %copy.48), channel_id=1, source_target_pairs={{0,1},{1,2},{2,3},{3,0},{4,5},{5,6},{6,7},{7,4},{8,9},{9,10},{10,1... | collective-permute-start | bytes 20744 | tf_op jit(solution)/shard_map/ppermute | solution.py:13
  21.0 15.1 %collective-permute-start.5 = (f32[16,6,18,1]{2,0,3,1:T(8,128)S(1)}, f32[16,6,18,1]{2,0,3,1:T(8,128)S(1)}, u32[]{:S(2)}, u32[]{:S(2)}) collective-permute-start(f32[16,6,18,1]{2,0,3,1:T(8,128)S(1)} %copy.50), channel_id=1, source_target_pairs={{1,0},{2,1},{3,2},{0,3},{5,4},{6,5},{7,6},{4,7},{9,8},{10,9},{11,1... | collective-permute-start | bytes 20744 | tf_op jit(solution)/shard_map/ppermute | solution.py:16
  37.7 1.8 copy-start.26
  39.5 11.6 %copy-start = (f32[16,6,18,129]{3,0,2,1:T(8,128)}, f32[16,6,18,129]{3,0,2,1:T(8,128)S(1)}, u32[]{:S(2)}) copy-start(f32[16,6,18,129]{3,0,2,1:T(8,128)S(1)} %get-tuple-element.28) | copy-start | bytes 2674948
  48.2 1.9 copy-start.11
  48.2 1.9 copy-start.12
  48.2 1.9 copy-start.23
  48.2 1.9 copy-start.24
  48.2 1.9 copy-start.25
  50.1 1.0 copy-start.9
  50.1 1.2 copy-start.17
  50.1 1.3 copy-start.18
  50.2 1.5 copy-start.19
  51.6 40.1 %copy-start.28 = (f32[16]{0:T(128)S(1)}, f32[16]{0:T(128)}, u32[]{:S(2)}) copy-start(f32[16]{0:T(128)} %param.7) | copy-start | bytes 196
  51.6 40.1 %copy-start.29 = (f32[16]{0:T(128)S(1)}, f32[16]{0:T(128)}, u32[]{:S(2)}) copy-start(f32[16]{0:T(128)} %param.8) | copy-start | bytes 196
  52.8 81.8 %copy-start.4 = (f32[16,4,16,128]{3,0,2,1:T(8,128)}, f32[16,4,16,128]{3,0,2,1:T(8,128)S(1)}, u32[]{:S(2)}) copy-start(f32[16,4,16,128]{3,0,2,1:T(8,128)S(1)} %get-tuple-element.47) | copy-start | bytes 1572868
  134.6 3.7 %copy-start.30 = (f32[16]{0:T(128)}, f32[16]{0:T(128)S(1)}, u32[]{:S(2)}) copy-start(f32[16]{0:T(128)S(1)} %get-tuple-element.16) | copy-start | bytes 196
  134.6 3.7 %copy-start.31 = (f32[16]{0:T(128)}, f32[16]{0:T(128)S(1)}, u32[]{:S(2)}) copy-start(f32[16]{0:T(128)S(1)} %get-tuple-element.17) | copy-start | bytes 196
  136.0 2.3 copy-start.1
  137.5 2.5 copy-start.8
  145.0 2.5 copy-start.3
  152.7 2.5 copy-start.6
  255.6 7.6 %collective-permute-start.6 = (f32[16,1,16,128]{3,0,2,1:T(8,128)}, f32[16,1,16,128]{3,0,2,1:T(8,128)S(1)}, u32[]{:S(2)}, u32[]{:S(2)}) collective-permute-start(f32[16,1,16,128]{3,0,2,1:T(8,128)} %get-tuple-element.35), channel_id=1, source_target_pairs={{0,16},{16,0},{1,17},{17,1},{2,18},{18,2},{3,19},{19,3},{4,20},{20... | collective-permute-start | bytes 393224 | tf_op jit(solution)/shard_map/ppermute | solution.py:13
  255.6 6.2 %copy-start.27 = (f32[16,16,3,3,3]{1,0,4,3,2:T(8,128)S(1)}, f32[16,16,3,3,3]{1,0,4,3,2:T(8,128)}, u32[]{:S(2)}) copy-start(f32[16,16,3,3,3]{1,0,4,3,2:T(8,128)} %param.6) | copy-start | bytes 82948
  255.6 8.8 %collective-permute-start.7 = (f32[16,1,16,128]{3,0,2,1:T(8,128)}, f32[16,1,16,128]{3,0,2,1:T(8,128)S(1)}, u32[]{:S(2)}, u32[]{:S(2)}) collective-permute-start(f32[16,1,16,128]{3,0,2,1:T(8,128)} %get-tuple-element.36), channel_id=1, source_target_pairs={{16,0},{0,16},{17,1},{1,17},{18,2},{2,18},{19,3},{3,19},{20,4},{4,... | collective-permute-start | bytes 393224 | tf_op jit(solution)/shard_map/ppermute | solution.py:16
  264.4 4.7 %collective-permute-start.9 = (f32[16,6,1,128]{3,0,2,1:T(8,128)S(1)}, f32[16,6,1,128]{3,0,2,1:T(8,128)S(1)}, u32[]{:S(2)}, u32[]{:S(2)}) collective-permute-start(f32[16,6,1,128]{3,0,2,1:T(8,128)S(1)} %get-tuple-element.32), channel_id=1, source_target_pairs={{4,0},{8,4},{12,8},{0,12},{5,1},{9,5},{13,9},{1,13},{6,2},{10,6},{... | collective-permute-start | bytes 147464 | tf_op jit(solution)/shard_map/ppermute | solution.py:16
  264.5 5.9 %collective-permute-start.8 = (f32[16,6,1,128]{3,0,2,1:T(8,128)S(1)}, f32[16,6,1,128]{3,0,2,1:T(8,128)S(1)}, u32[]{:S(2)}, u32[]{:S(2)}) collective-permute-start(f32[16,6,1,128]{3,0,2,1:T(8,128)S(1)} %get-tuple-element.31), channel_id=1, source_target_pairs={{0,4},{4,8},{8,12},{12,0},{1,5},{5,9},{9,13},{13,1},{2,6},{6,10},{... | collective-permute-start | bytes 147464 | tf_op jit(solution)/shard_map/ppermute | solution.py:13
  273.5 9.7 %collective-permute-start.10 = (f32[16,6,18,1]{2,0,3,1:T(8,128)S(1)}, f32[16,6,18,1]{2,0,3,1:T(8,128)S(1)}, u32[]{:S(2)}, u32[]{:S(2)}) collective-permute-start(f32[16,6,18,1]{2,0,3,1:T(8,128)S(1)} %copy.56), channel_id=1, source_target_pairs={{1,0},{2,1},{3,2},{0,3},{5,4},{6,5},{7,6},{4,7},{9,8},{10,9},{11,1... | collective-permute-start | bytes 20744 | tf_op jit(solution)/shard_map/ppermute | solution.py:16
  274.2 10.6 %collective-permute-start.11 = (f32[16,6,18,1]{2,0,3,1:T(8,128)S(1)}, f32[16,6,18,1]{2,0,3,1:T(8,128)S(1)}, u32[]{:S(2)}, u32[]{:S(2)}) collective-permute-start(f32[16,6,18,1]{2,0,3,1:T(8,128)S(1)} %copy.60), channel_id=1, source_target_pairs={{0,1},{1,2},{2,3},{3,0},{4,5},{5,6},{6,7},{7,4},{8,9},{9,10},{10,1... | collective-permute-start | bytes 20744 | tf_op jit(solution)/shard_map/ppermute | solution.py:13
  297.0 2.3 copy-start.10
  297.0 2.3 copy-start.13
  297.0 2.3 copy-start.20
  297.3 2.1 copy-start.21
  297.3 2.1 copy-start.22
  299.3 1.1 copy-start.14
  299.4 1.2 copy-start.15
  299.4 1.3 copy-start.16
